TPU v7x, 32 devices: a whole 2x2x4 slice. The times are simulated.
32 devices in a mesh: batch: 8 (over z, x), seq: 4 (over y, core).
Axes of the slice: x: 2, y: 2, z: 4, core: 2. Of those that a mesh axis runs over, the one named last changes fastest.
Arguments:
- tokens: bfloat16 [8, 1024, 1024], P('batch', 'seq'), may hold values from -6 to 6
- cotangent: bfloat16 [8, 1024, 1024], P('batch', 'seq'), may hold values from -6 to 6
- image_tokens: bfloat16 [8, 1025, 768], P('batch'), may hold values from -6 to 6
- image_lengths: int32 [8], P('batch'), may hold values from 512 to 1025, as said below
- key_mask: int32 [8, 1025], P('batch'), may hold values 0 or 1
- camera: bfloat16 [8, 1024], P(None, 'batch'), may hold values from -6 to 6
- modulation: bfloat16 [1024, 6144], P('batch'), may hold values from -0.1875 to 0.1875
- q_cross: bfloat16 [1024, 1024], P('batch'), may hold values from -0.1875 to 0.1875
- kv_image: bfloat16 [768, 2048], P('batch'), may hold values from -0.21875 to 0.21875
- out_cross: bfloat16 [1024, 1024], P('batch'), may hold values from -3.5 to 3.5
- qkv_self: bfloat16 [1024, 3072], P('batch'), may hold values from -0.1875 to 0.1875
- out_self: bfloat16 [1024, 1024], P('batch'), may hold values from -6 to 6
- mlp_in: bfloat16 [1024, 4096], P('batch'), may hold values from -0.1875 to 0.1875
- mlp_out: bfloat16 [4096, 1024], P('batch'), may hold values from -0.09375 to 0.09375
Outputs:
- output: bfloat16 [8, 1024, 1024], P('batch', 'seq')
- grad_tokens: float32 [8, 1024, 1024], P('batch', 'seq')
- grad_modulation: float32 [1024, 6144], P('batch')
- grad_q_cross: float32 [1024, 1024], P('batch')
- grad_kv_image: float32 [768, 2048], P('batch')
- grad_out_cross: float32 [1024, 1024], P('batch')
- grad_qkv_self: float32 [1024, 3072], P('batch')
- grad_out_self: float32 [1024, 1024], P('batch')
- grad_mlp_in: float32 [1024, 4096], P('batch')
- grad_mlp_out: float32 [4096, 1024], P('batch')
Inputs may be any that keep to these rules, and one draw needn't show every extreme that they name: `image_lengths`: some object has 1025 valid image tokens and some has 512.
All inputs are finite; a program needn't handle non-finite values. No bound on the sum of `key_mask` on one device may be relied on, other than what follows from the above.
Results may differ from a plain program's by a relative error of at most 0.025.
The roundings to bfloat16 on the way count: a program that leaves them out, or rounds other values in their place, can miss the bound.
Values may be sent and summed in bfloat16 or wider, within the bound.
A program may use at most 256 MiB of HBM per device.

v0:
```python
import jax
import jax.numpy as jnp
from jax import lax
from jax.sharding import PartitionSpec as P

HEADS = 16
HEAD_DIM = 64
epsilon = 1e-06
group_heads = 4
highest = lax.Precision.HIGHEST


def modulated_norm(values, shift, scale):
    center = values - jnp.mean(values, axis=-1, keepdims=True)
    normed = center * lax.rsqrt(jnp.mean(center * center, axis=-1, keepdims=True) + epsilon)
    return normed * (1.0 + scale) + shift


def product(left, right):
    return jnp.dot(left, right, preferred_element_type=jnp.float32)


def contract_rows(left, right):
    return lax.dot_general(
        left, right, (((0,), (0,)), ((), ())), preferred_element_type=jnp.float32
    )


def times_transposed(left, right):
    return lax.dot_general(
        left, right, (((1,), (1,)), ((), ())), preferred_element_type=jnp.float32
    )


def split_heads(values):
    rows = values.shape[0]
    grouped = values.reshape(rows, HEADS // group_heads, group_heads, HEAD_DIM)
    return grouped.transpose(1, 2, 0, 3)


def join_heads(values):
    groups, inner, rows, depth = values.shape
    return values.transpose(2, 0, 1, 3).reshape(rows, groups * inner * depth)


def scores_of(query_group, key_group, valid):
    scores = jnp.einsum(
        "hqd,hkd->hqk", query_group, key_group, preferred_element_type=jnp.float32
    ) * HEAD_DIM ** (-0.5)
    return jnp.where(valid[None, None, :], scores, -1000000000.0)


def attend_forward(query, key_rows, value_rows, valid):

    def one_group(pieces):
        query_group, key_group, value_group = pieces
        scores = scores_of(query_group, key_group, valid)
        top = jnp.max(scores, axis=-1, keepdims=True)
        expo = jnp.exp(scores - top)
        total = jnp.sum(expo, axis=-1, keepdims=True)
        probs = (expo / total).astype(jnp.bfloat16)
        result = jnp.einsum("hqk,hkd->hqd", probs, value_group, preferred_element_type=jnp.float32)
        return (result, top, total)

    results, tops, totals = lax.map(
        one_group, (split_heads(query), split_heads(key_rows), split_heads(value_rows))
    )
    return (join_heads(results), (tops, totals))


def attend_backward(query, key_rows, value_rows, valid, stats, grad_output):
    tops, totals = stats

    def one_group(pieces):
        query_group, key_group, value_group, top, total, grad_group = pieces
        scores = scores_of(query_group, key_group, valid)
        probs = jnp.exp(scores - top) / total
        grad_probs = jnp.einsum(
            "hqd,hkd->hqk", grad_group, value_group, preferred_element_type=jnp.float32
        )
        inner = jnp.sum(probs * grad_probs, axis=-1, keepdims=True)
        grad_scores = (probs * (grad_probs - inner)).astype(jnp.bfloat16)
        factor = HEAD_DIM ** (-0.5)
        grad_query = (
            jnp.einsum("hqk,hkd->hqd", grad_scores, key_group, preferred_element_type=jnp.float32)
            * factor
        )
        grad_keys = (
            jnp.einsum("hqk,hqd->hkd", grad_scores, query_group, preferred_element_type=jnp.float32)
            * factor
        )
        grad_values = jnp.einsum(
            "hqk,hqd->hkd",
            probs.astype(jnp.bfloat16),
            grad_group,
            preferred_element_type=jnp.float32,
        )
        return (grad_query, inner, grad_keys, grad_values)

    results = lax.map(
        one_group,
        (
            split_heads(query),
            split_heads(key_rows),
            split_heads(value_rows),
            tops,
            totals,
            split_heads(grad_output),
        ),
    )
    return (join_heads(results[0]), results[1], join_heads(results[2]), join_heads(results[3]))


def local(
    tokens,
    cotangent,
    image_tokens,
    image_lengths,
    key_mask,
    camera,
    modulation,
    q_cross,
    kv_image,
    out_cross,
    qkv_self,
    out_self,
    mlp_in,
    mlp_out,
):
    q_full, kv_full, out_cross_full, qkv_full, out_self_full, mlp_in_full, mlp_out_full = (
        lax.all_gather(q_cross, "batch", axis=0, tiled=True),
        lax.all_gather(kv_image, "batch", axis=0, tiled=True),
        lax.all_gather(out_cross, "batch", axis=0, tiled=True),
        lax.all_gather(qkv_self, "batch", axis=0, tiled=True),
        lax.all_gather(out_self, "batch", axis=0, tiled=True),
        lax.all_gather(mlp_in, "batch", axis=0, tiled=True),
        lax.all_gather(mlp_out, "batch", axis=0, tiled=True),
    )
    camera_gate = jax.nn.silu(camera.astype(jnp.float32)).astype(jnp.bfloat16)
    modulation_all = lax.psum(product(camera_gate, modulation), "batch")
    object_index = lax.axis_index("batch")
    width = tokens.shape[2]
    shifts = lax.dynamic_index_in_dim(modulation_all, object_index, 0, keepdims=False).reshape(
        6, width
    )
    stream = tokens[0].astype(jnp.float32)
    image_rows = image_tokens[0]
    positions = jnp.arange(image_rows.shape[0], dtype=jnp.int32)
    valid = (positions < image_lengths[0]) & ((key_mask[0] == 1) | (positions == 0))
    everywhere = jnp.ones((lax.axis_size("seq") * stream.shape[0],), dtype=jnp.bool_)
    normed_cross, cross_pullback = jax.vjp(modulated_norm, stream, shifts[0], shifts[1])
    normed_cross = normed_cross.astype(jnp.bfloat16)
    query_cross = product(normed_cross, q_full).astype(jnp.bfloat16)
    image_kv = product(image_rows, kv_full)
    image_keys = image_kv[:, :width].astype(jnp.bfloat16)
    image_values = image_kv[:, width:].astype(jnp.bfloat16)
    attended_cross, cross_stats = attend_forward(query_cross, image_keys, image_values, valid)
    attended_cross = attended_cross.astype(jnp.bfloat16)
    after_cross = stream + product(attended_cross, out_cross_full)
    normed_self, self_pullback = jax.vjp(modulated_norm, after_cross, shifts[2], shifts[3])
    normed_self = normed_self.astype(jnp.bfloat16)
    packed = product(normed_self, qkv_full).astype(jnp.bfloat16)
    query_self = packed[:, :width]
    key_local = packed[:, width : 2 * width]
    value_local = packed[:, 2 * width :]
    key_whole, value_whole = (
        lax.all_gather(key_local, "seq", axis=0, tiled=True),
        lax.all_gather(value_local, "seq", axis=0, tiled=True),
    )
    attended_self, self_stats = attend_forward(query_self, key_whole, value_whole, everywhere)
    attended_self = attended_self.astype(jnp.bfloat16)
    after_self = after_cross + product(attended_self, out_self_full)
    normed_mlp, mlp_pullback = jax.vjp(modulated_norm, after_self, shifts[4], shifts[5])
    normed_mlp = normed_mlp.astype(jnp.bfloat16)
    up_rows = product(normed_mlp, mlp_in_full)
    hidden, gelu_pullback = jax.vjp(jax.nn.gelu, up_rows)
    hidden = hidden.astype(jnp.bfloat16)
    output = after_self + product(hidden, mlp_out_full)
    grad_stream = cotangent[0].astype(jnp.float32)
    grad_branch = grad_stream.astype(jnp.bfloat16)
    grad_mlp_out = contract_rows(hidden, grad_branch)
    (grad_up,) = gelu_pullback(times_transposed(grad_branch, mlp_out_full))
    grad_up = grad_up.astype(jnp.bfloat16)
    grad_mlp_in = contract_rows(normed_mlp, grad_up)
    grad_from, shift_mlp, scale_mlp = mlp_pullback(times_transposed(grad_up, mlp_in_full))
    grad_stream = grad_stream + grad_from
    grad_branch = grad_stream.astype(jnp.bfloat16)
    grad_out_self = contract_rows(attended_self, grad_branch)
    grad_attended = times_transposed(grad_branch, out_self_full).astype(jnp.bfloat16)
    grad_query, inner_local, key_terms, value_terms = attend_backward(
        query_self, key_whole, value_whole, everywhere, self_stats, grad_attended
    )
    grad_key, grad_value = (
        lax.psum_scatter(key_terms, "seq", scatter_dimension=0, tiled=True),
        lax.psum_scatter(value_terms, "seq", scatter_dimension=0, tiled=True),
    )
    grad_packed = jnp.concatenate([grad_query, grad_key, grad_value], axis=1).astype(jnp.bfloat16)
    grad_qkv_self = contract_rows(normed_self, grad_packed)
    grad_from, shift_self, scale_self = self_pullback(times_transposed(grad_packed, qkv_full))
    grad_stream = grad_stream + grad_from
    grad_branch = grad_stream.astype(jnp.bfloat16)
    grad_out_cross = contract_rows(attended_cross, grad_branch)
    grad_attended = times_transposed(grad_branch, out_cross_full).astype(jnp.bfloat16)
    grad_query, inner_cross, key_terms, value_terms = attend_backward(
        query_cross, image_keys, image_values, valid, cross_stats, grad_attended
    )
    image_float = image_rows.astype(jnp.float32)
    image_key_grad, image_value_grad = (
        lax.psum_scatter(
            key_terms.astype(jnp.bfloat16), "seq", scatter_dimension=1, tiled=True
        ).astype(jnp.float32),
        lax.psum_scatter(
            value_terms.astype(jnp.bfloat16), "seq", scatter_dimension=1, tiled=True
        ).astype(jnp.float32),
    )
    block_width = image_key_grad.shape[1]
    column_start = lax.axis_index("seq") * block_width
    image_grads = jnp.concatenate([image_key_grad, image_value_grad], axis=1)
    kv_block = lax.dot_general(
        image_float,
        image_grads,
        (((0,), (0,)), ((), ())),
        precision=highest,
        preferred_element_type=jnp.float32,
    )
    grad_kv_image = jnp.zeros((image_rows.shape[1], 2 * width), jnp.float32)
    grad_kv_image = lax.dynamic_update_slice(
        grad_kv_image, kv_block[:, :block_width], (jnp.int32(0), column_start)
    )
    grad_kv_image = lax.dynamic_update_slice(
        grad_kv_image, kv_block[:, block_width:], (jnp.int32(0), column_start + width)
    )
    grad_query = grad_query.astype(jnp.bfloat16)
    grad_q_cross = contract_rows(normed_cross, grad_query)
    grad_from, shift_cross, scale_cross = cross_pullback(times_transposed(grad_query, q_full))
    grad_input = grad_stream + grad_from
    grad_row = jnp.concatenate(
        [shift_cross, scale_cross, shift_self, scale_self, shift_mlp, scale_mlp]
    )
    grad_table = lax.dynamic_update_slice(
        jnp.zeros(modulation_all.shape, jnp.float32),
        grad_row[None, :],
        (object_index, jnp.int32(0)),
    )
    grad_table = lax.psum(grad_table, ("batch", "seq"))
    grad_modulation = lax.dot_general(
        camera_gate.astype(jnp.float32),
        grad_table,
        (((0,), (0,)), ((), ())),
        precision=highest,
        preferred_element_type=jnp.float32,
    )
    terms = (
        grad_q_cross,
        grad_kv_image,
        grad_out_cross,
        grad_qkv_self,
        grad_out_self,
        grad_mlp_in,
        grad_mlp_out,
    )
    shares = (
        lax.psum_scatter(
            terms[0].astype(jnp.bfloat16), "batch", scatter_dimension=0, tiled=True
        ).astype(jnp.float32),
        lax.psum_scatter(
            terms[1].astype(jnp.bfloat16), "batch", scatter_dimension=0, tiled=True
        ).astype(jnp.float32),
        lax.psum_scatter(
            terms[2].astype(jnp.bfloat16), "batch", scatter_dimension=0, tiled=True
        ).astype(jnp.float32),
        lax.psum_scatter(
            terms[3].astype(jnp.bfloat16), "batch", scatter_dimension=0, tiled=True
        ).astype(jnp.float32),
        lax.psum_scatter(
            terms[4].astype(jnp.bfloat16), "batch", scatter_dimension=0, tiled=True
        ).astype(jnp.float32),
        lax.psum_scatter(
            terms[5].astype(jnp.bfloat16), "batch", scatter_dimension=0, tiled=True
        ).astype(jnp.float32),
        lax.psum_scatter(
            terms[6].astype(jnp.bfloat16), "batch", scatter_dimension=0, tiled=True
        ).astype(jnp.float32),
    )
    totals = (
        lax.psum(shares[0].astype(jnp.bfloat16), "seq").astype(jnp.float32),
        lax.psum(shares[1].astype(jnp.bfloat16), "seq").astype(jnp.float32),
        lax.psum(shares[2].astype(jnp.bfloat16), "seq").astype(jnp.float32),
        lax.psum(shares[3].astype(jnp.bfloat16), "seq").astype(jnp.float32),
        lax.psum(shares[4].astype(jnp.bfloat16), "seq").astype(jnp.float32),
        lax.psum(shares[5].astype(jnp.bfloat16), "seq").astype(jnp.float32),
        lax.psum(shares[6].astype(jnp.bfloat16), "seq").astype(jnp.float32),
    )
    return (
        output.astype(jnp.bfloat16)[None],
        grad_input[None],
        grad_modulation,
        totals[0],
        totals[1],
        totals[2],
        totals[3],
        totals[4],
        totals[5],
        totals[6],
    )


def solution(mesh):
    return jax.shard_map(
        local,
        mesh=mesh,
        in_specs=(
            P("batch", "seq", None),
            P("batch", "seq", None),
            P("batch", None, None),
            P("batch"),
            P("batch", None),
            P(None, "batch"),
            P("batch", None),
            P("batch", None),
            P("batch", None),
            P("batch", None),
            P("batch", None),
            P("batch", None),
            P("batch", None),
            P("batch", None),
        ),
        out_specs=(
            P("batch", "seq", None),
            P("batch", "seq", None),
            P("batch", None),
            P("batch", None),
            P("batch", None),
            P("batch", None),
            P("batch", None),
            P("batch", None),
            P("batch", None),
            P("batch", None),
        ),
        check_vma=False,
    )
```

profile of v0, /device:TPU:0, one launch (start us, length us, event | category | flops | bytes accessed | tf_op | source)
XLA Modules:
  0.0 1926.2 jit_solution(18248695921334428257)
XLA Ops:
  15.5 69.2 %all-reduce.5.cloned.1.call-done = f32[8,6144]{1,0:T(8,128)} async-done(((f32[8,6144]{1,0:T(8,128)}), f32[8,6144]{1,0:T(8,128)}) %all-reduce.5.cloned.1.call-update) | async-done | bytes 196624 | tf_op jit(solution)/shard_map/psum | solution.py:140
  85.7 49.7 %all-gather.10.cloned.1.call-done = bf16[1024,1024]{1,0:T(8,128)(2,1)} async-done(((bf16[128,1024]{1,0:T(8,128)(2,1)}), bf16[1024,1024]{1,0:T(8,128)(2,1)}) %all-gather.10.cloned.1.call-update) | async-done | bytes 2097168 | tf_op jit(solution)/shard_map/all_gather | solution.py:131
  138.0 58.8 %all-gather.12.cloned.1.call-done = bf16[768,2048]{1,0:T(8,128)(2,1)} async-done(((bf16[96,2048]{1,0:T(8,128)(2,1)}), bf16[768,2048]{1,0:T(8,128)(2,1)}) %all-gather.12.cloned.1.call-update) | async-done | bytes 3145744 | tf_op jit(solution)/shard_map/all_gather | solution.py:132
  213.2 18.4 while.56
  249.9 96.9 %all-gather.16.cloned.1.call-done = bf16[1024,3072]{1,0:T(8,128)(2,1)} async-done(((bf16[128,3072]{1,0:T(8,128)(2,1)}), bf16[1024,3072]{1,0:T(8,128)(2,1)}) %all-gather.16.cloned.1.call-update) | async-done | bytes 6291472 | tf_op jit(solution)/shard_map/all_gather | solution.py:134
  377.6 20.9 %all-gather.20.cloned.1.call-done = bf16[1024,1024]{1,0:T(8,128)(2,1)} async-done(((bf16[256,1024]{1,0:T(8,128)(2,1)}), bf16[1024,1024]{1,0:T(8,128)(2,1)}) %all-gather.20.cloned.1.call-update) | async-done | bytes 2097168 | tf_op jit(solution)/shard_map/all_gather | solution.py:168
  403.3 23.0 %while.57 = (s32[]{:T(128)}, bf16[4,4,256,64]{2,3,1,0:T(8,128)(2,1)}, f32[4,4,256,1]{2,1,3,0:T(4,128)S(1)}, f32[4,4,256,1]{2,1,3,0:T(4,128)S(1)}, bf16[4,4,256,6...) while((s32[]{:T(128)}, ...), condition=%wide.region_12.13_spmd, body=%wide.region_9.12_spmd.sunk | while | flops 277870592 | bytes 18258072 | solution.py:65
  426.2 24.1 %all-gather.22.cloned.1.call-done = bf16[1024,1024]{1,0:T(8,128)(2,1)} async-done(((bf16[128,1024]{1,0:T(8,128)(2,1)}), bf16[1024,1024]{1,0:T(8,128)(2,1)}) %all-gather.22.cloned.1.call-update) | async-done | bytes 2097168 | tf_op jit(solution)/shard_map/all_gather | solution.py:135
  454.2 122.0 %all-gather.24.cloned.1.call-done = bf16[1024,4096]{1,0:T(8,128)(2,1)} async-done(((bf16[128,4096]{1,0:T(8,128)(2,1)}), bf16[1024,4096]{1,0:T(8,128)(2,1)}) %all-gather.24.cloned.1.call-update) | async-done | bytes 8388624 | tf_op jit(solution)/shard_map/all_gather | solution.py:136
  584.3 117.2 %all-gather.26.cloned.1.call-done = bf16[4096,1024]{1,0:T(8,128)(2,1)} async-done(((bf16[512,1024]{1,0:T(8,128)(2,1)}), bf16[4096,1024]{1,0:T(8,128)(2,1)}) %all-gather.26.cloned.1.call-update) | async-done | bytes 8388624 | tf_op jit(solution)/shard_map/all_gather | solution.py:137
  720.9 39.8 %while.58 = (s32[]{:T(128)}, bf16[4,4,256,64]{2,3,1,0:T(8,128)(2,1)}, f32[4,4,1024,64]{2,3,1,0:T(8,128)}, f32[4,4,1024,64]{2,3,1,0:T(8,128)}, bf16[4,4,256,64]{2...) while((s32[]{:T(128)}, ...), condition=%wide.region_19.20_spmd, body=%wide.region_17.19_spmd.sunk | while | flops 680852480 | bytes 48534732 | solution.py:100
  761.4 42.2 %reduce-scatter.14.cloned.1.call-done = f32[256,1024]{0,1:T(8,128)} async-done(((f32[1024,1024]{0,1:T(8,128)}), f32[256,1024]{0,1:T(8,128)}) %reduce-scatter.14.cloned.1.call-update) | async-done | bytes 1048592 | tf_op jit(solution)/shard_map/reduce_scatter | solution.py:195
  804.9 45.6 %reduce-scatter.12.cloned.1.call-done = f32[256,1024]{0,1:T(8,128)} async-done(((f32[1024,1024]{0,1:T(8,128)}), f32[256,1024]{0,1:T(8,128)}) %reduce-scatter.12.cloned.1.call-update) | async-done | bytes 1048592 | tf_op jit(solution)/shard_map/reduce_scatter | solution.py:194
  863.9 40.3 %while.59 = (s32[]{:T(128)}, bf16[4,4,256,64]{2,3,1,0:T(8,128)(2,1)}, bf16[4,4,1025,64]{2,3,1,0:T(8,128)(2,1)}, bf16[4,4,1025,64]{2,3,1,0:T(8,128)(2,1)}, pred[1...) while((s32[]{:T(128)}, ...), condition=%wide.region_26.27_spmd, body=%wide.region_24.26_spmd.sunk | while | flops 682566912 | bytes 82707776 | solution.py:100
  937.4 35.5 %reduce-scatter.18.cloned.1.call-done = bf16[1025,256]{0,1:T(8,128)(2,1)} async-done(((bf16[1025,1024]{0,1:T(8,128)(2,1)}), bf16[1025,256]{0,1:T(8,128)(2,1)}) %reduce-scatter.18.cloned.1.call-update) | async-done | bytes 524816 | tf_op jit(solution)/shard_map/reduce_scatter | solution.py:209
  995.6 48.8 %reduce-scatter.28.cloned.1.call-done = bf16[128,1024]{1,0:T(8,128)(2,1)} async-done(((bf16[1024,1024]{1,0:T(8,128)(2,1)}), bf16[128,1024]{1,0:T(8,128)(2,1)}) %reduce-scatter.28.cloned.1.call-update) | async-done | bytes 262160 | tf_op jit(solution)/shard_map/reduce_scatter | solution.py:275
  1044.4 71.2 %reduce-scatter.16.cloned.1.call-done = bf16[128,1024]{1,0:T(8,128)(2,1)} async-done(((bf16[1024,1024]{1,0:T(8,128)(2,1)}), bf16[128,1024]{1,0:T(8,128)(2,1)}) %reduce-scatter.16.cloned.1.call-update) | async-done | bytes 262160 | tf_op jit(solution)/shard_map/reduce_scatter | solution.py:263
  1115.6 71.3 %reduce-scatter.24.cloned.1.call-done = bf16[128,1024]{1,0:T(8,128)(2,1)} async-done(((bf16[1024,1024]{1,0:T(8,128)(2,1)}), bf16[128,1024]{1,0:T(8,128)(2,1)}) %reduce-scatter.24.cloned.1.call-update) | async-done | bytes 262160 | tf_op jit(solution)/shard_map/reduce_scatter | solution.py:269
  1186.9 152.0 %reduce-scatter.30.cloned.1.call-done = bf16[128,4096]{1,0:T(8,128)(2,1)} async-done(((bf16[1024,4096]{1,0:T(8,128)(2,1)}), bf16[128,4096]{1,0:T(8,128)(2,1)}) %reduce-scatter.30.cloned.1.call-update) | async-done | bytes 1048592 | tf_op jit(solution)/shard_map/reduce_scatter | solution.py:278
  1338.9 151.7 %reduce-scatter.32.cloned.1.call-done = bf16[512,1024]{1,0:T(8,128)(2,1)} async-done(((bf16[4096,1024]{1,0:T(8,128)(2,1)}), bf16[512,1024]{1,0:T(8,128)(2,1)}) %reduce-scatter.32.cloned.1.call-update) | async-done | bytes 1048592 | tf_op jit(solution)/shard_map/reduce_scatter | solution.py:281
  1490.6 77.8 %reduce-scatter.22.cloned.1.call-done = bf16[96,2048]{1,0:T(8,128)(2,1)} async-done(((bf16[768,2048]{1,0:T(8,128)(2,1)}), bf16[96,2048]{1,0:T(8,128)(2,1)}) %reduce-scatter.22.cloned.1.call-update) | async-done | bytes 393232 | tf_op jit(solution)/shard_map/reduce_scatter | solution.py:266
  1568.4 121.2 %reduce-scatter.26.cloned.1.call-done = bf16[128,3072]{1,0:T(8,128)(2,1)} async-done(((bf16[1024,3072]{1,0:T(8,128)(2,1)}), bf16[128,3072]{1,0:T(8,128)(2,1)}) %reduce-scatter.26.cloned.1.call-update) | async-done | bytes 786448 | tf_op jit(solution)/shard_map/reduce_scatter | solution.py:272
  1699.4 119.4 %all-reduce.7.cloned.1.call-done = f32[8,6144]{1,0:T(8,128)} async-done(((f32[8,6144]{1,0:T(8,128)}), f32[8,6144]{1,0:T(8,128)}) %all-reduce.7.cloned.1.call-update) | async-done | bytes 196624 | tf_op jit(solution)/shard_map/psum | solution.py:245
  1822.9 84.5 %all-reduce.9.cloned.1.call-done = (bf16[128,1024]{1,0:T(8,128)(2,1)}, bf16[96,2048]{1,0:T(8,128)(2,1)}, bf16[128,1024]{1,0:T(8,128)(2,1)}, bf16[128,3072]{1,0:T...) async-done(((bf16[128,1024]{1,0:T(8,128)(2,1)}, bf16[96,2048]{1,0:T(8,128)(2,1)}, bf16[128,1024]{1,0:T(8,128)(2,1)}, ...) | async-done | bytes 4063248 | tf_op jit(solution)/shard_map/psum | solution.py:286
  (443 shorter events, 328.9 us)
Async XLA Ops:
  7.2 77.5 %all-reduce.5.cloned.1.call-start = ((), (), s32[]{:S(2)}) async-start(), calls=%async_computation.11 | async-start | bytes 393216 | tf_op jit(solution)/shard_map/psum | solution.py:140
  9.8 125.6 %all-gather.10.cloned.1.call-start = ((), (), s32[]{:S(2)}) async-start(), calls=%async_computation.12 | async-start | bytes 2359296 | tf_op jit(solution)/shard_map/all_gather | solution.py:131
  10.6 186.2 %all-gather.12.cloned.1.call-start = ((), (), s32[]{:S(2)}) async-start(), calls=%async_computation.13 | async-start | bytes 3538944 | tf_op jit(solution)/shard_map/all_gather | solution.py:132
  11.3 235.6 %all-gather.14.cloned.1.call-start = ((), (), s32[]{:S(2)}) async-start(), calls=%async_computation.14 | async-start | bytes 2359296 | tf_op jit(solution)/shard_map/all_gather | solution.py:133
  11.9 334.9 %all-gather.16.cloned.1.call-start = ((), (), s32[]{:S(2)}) async-start(), calls=%async_computation.15 | async-start | bytes 7077888 | tf_op jit(solution)/shard_map/all_gather | solution.py:134
  12.5 361.1 %all-gather.18.cloned.1.call-start = ((), (), s32[]{:S(2)}) async-start(), calls=%async_computation.16 | async-start | bytes 2621440 | tf_op jit(solution)/shard_map/all_gather | solution.py:167
  352.7 45.8 %all-gather.20.cloned.1.call-start = ((), (), s32[]{:S(2)}) async-start(), calls=%async_computation.17 | async-start | bytes 2621440 | tf_op jit(solution)/shard_map/all_gather | solution.py:168
  353.4 96.9 %all-gather.22.cloned.1.call-start = ((), (), s32[]{:S(2)}) async-start(), calls=%async_computation.18 | async-start | bytes 2359296 | tf_op jit(solution)/shard_map/all_gather | solution.py:135
  354.2 222.0 %all-gather.24.cloned.1.call-start = ((), (), s32[]{:S(2)}) async-start(), calls=%async_computation.19 | async-start | bytes 9437184 | tf_op jit(solution)/shard_map/all_gather | solution.py:136
  354.9 346.6 %all-gather.26.cloned.1.call-start = ((), (), s32[]{:S(2)}) async-start(), calls=%async_computation.20 | async-start | bytes 9437184 | tf_op jit(solution)/shard_map/all_gather | solution.py:137
  355.5 448.1 %reduce-scatter.14.cloned.1.call-start = ((), (), s32[]{:S(2)}) async-start(), calls=%async_computation.22 | async-start | bytes 5242880 | tf_op jit(solution)/shard_map/reduce_scatter | solution.py:195
  760.8 89.7 %reduce-scatter.12.cloned.1.call-start = ((), (), s32[]{:S(2)}) async-start(), calls=%async_computation.21 | async-start | bytes 5242880 | tf_op jit(solution)/shard_map/reduce_scatter | solution.py:194
  761.3 176.1 %reduce-scatter.20.cloned.1.call-start = ((), (), s32[]{:S(2)}) async-start(), calls=%async_computation.26 | async-start | bytes 2949120 | tf_op jit(solution)/shard_map/reduce_scatter | solution.py:212
  904.3 68.7 %reduce-scatter.18.cloned.1.call-start = ((), (), s32[]{:S(2)}) async-start(), calls=%async_computation.25 | async-start | bytes 2949120 | tf_op jit(solution)/shard_map/reduce_scatter | solution.py:209
  904.9 139.5 %reduce-scatter.28.cloned.1.call-start = ((), (), s32[]{:S(2)}) async-start(), calls=%async_computation.30 | async-start | bytes 2359296 | tf_op jit(solution)/shard_map/reduce_scatter | solution.py:275
  908.2 207.4 %reduce-scatter.16.cloned.1.call-start = ((), (), s32[]{:S(2)}) async-start(), calls=%async_computation.24 | async-start | bytes 2359296 | tf_op jit(solution)/shard_map/reduce_scatter | solution.py:263
  911.8 275.1 %reduce-scatter.24.cloned.1.call-start = ((), (), s32[]{:S(2)}) async-start(), calls=%async_computation.28 | async-start | bytes 2359296 | tf_op jit(solution)/shard_map/reduce_scatter | solution.py:269
  915.5 423.4 %reduce-scatter.30.cloned.1.call-start = ((), (), s32[]{:S(2)}) async-start(), calls=%async_computation.31 | async-start | bytes 9437184 | tf_op jit(solution)/shard_map/reduce_scatter | solution.py:278
  923.3 567.3 %reduce-scatter.32.cloned.1.call-start = ((), (), s32[]{:S(2)}) async-start(), calls=%async_computation.32 | async-start | bytes 9437184 | tf_op jit(solution)/shard_map/reduce_scatter | solution.py:281
  932.0 636.4 %reduce-scatter.22.cloned.1.call-start = ((), (), s32[]{:S(2)}) async-start(), calls=%async_computation.27 | async-start | bytes 3538944 | tf_op jit(solution)/shard_map/reduce_scatter | solution.py:266
  982.9 706.8 %reduce-scatter.26.cloned.1.call-start = ((), (), s32[]{:S(2)}) async-start(), calls=%async_computation.29 | async-start | bytes 7077888 | tf_op jit(solution)/shard_map/reduce_scatter | solution.py:272
  989.3 700.4 %copy-start.5 = (f32[256,1024]{1,0:T(8,128)S(1)}, f32[256,1024]{1,0:T(8,128)}, u32[]{:S(2)}) copy-start(f32[256,1024]{1,0:T(8,128)} %copy-done.3) | copy-start | bytes 3145732
  989.3 829.5 %all-reduce.7.cloned.1.call-start = ((), (), s32[]{:S(2)}) async-start(), calls=%async_computation.23 | async-start | bytes 393216 | tf_op jit(solution)/shard_map/psum | solution.py:245
  995.5 911.8 %all-reduce.9.cloned.1.call-start = ((), (), s32[]{:S(2)}) async-start(), calls=%async_computation.33 | async-start | bytes 8126464 | tf_op jit(solution)/shard_map/psum | solution.py:286
  (106 other events, 4647.0 us)
Sparse Core Ops, SparseCore 0:
  11.9 72.7 all-reduce.4
  87.1 48.3 all-gather.9
  137.9 58.9 all-gather.11
  199.0 47.9 all-gather.13
  249.2 97.5 all-gather.15
  352.8 20.7 all-gather.17
  375.8 22.5 all-gather.19
  400.8 49.5 all-gather.21
  452.7 123.4 all-gather.23
  578.4 123.1 all-gather.25
  760.9 42.6 reduce-scatter.13
  806.0 44.4 reduce-scatter.11
  904.3 33.0 reduce-scatter.19
  939.8 33.0 reduce-scatter.17
  976.7 67.6 reduce-scatter.27
  1048.8 66.7 reduce-scatter.15
  1120.0 66.8 reduce-scatter.23
  1190.8 148.0 reduce-scatter.29
  1342.5 147.9 reduce-scatter.31
  1495.0 73.3 reduce-scatter.21
  1572.4 117.1 reduce-scatter.25
  1696.7 122.1 all-reduce.6
  1822.0 85.3 all-reduce.8
where the time goes:
time: 1940 us; the launch traced here: 1930 us
  waiting for transfers between devices  1620 us (84%)
  matrix products  195 us (10%)
  local copies, waits for them, and re-layouts  57.6 us (3%)
  other arithmetic  31.7 us (2%)
    reduce_scatter x1, waiting for transfers between devices, local(): lax.psum_scatter(terms[5].astype(jnp.bfloat16), 'batch', scatter_dimensio...  152 us
    reduce_scatter x1, waiting for transfers between devices, local(): lax.psum_scatter(terms[6].astype(jnp.bfloat16), 'batch', scatter_dimensio...  152 us
    all_gather x1, waiting for transfers between devices, local(): lax.all_gather(mlp_in, 'batch', axis=0, tiled=True)  122 us
    reduce_scatter x1, waiting for transfers between devices, local(): lax.psum_scatter(terms[3].astype(jnp.bfloat16), 'batch', scatter_dimensio...  121 us
    psum x1, waiting for transfers between devices, local(): grad_table = lax.psum(grad_table, ('batch', 'seq'))  119 us
    all_gather x1, waiting for transfers between devices, local(): lax.all_gather(mlp_out, 'batch', axis=0, tiled=True)  117 us
    all_gather x1, waiting for transfers between devices, local(): lax.all_gather(qkv_self, 'batch', axis=0, tiled=True)  96.9 us
    psum x1, waiting for transfers between devices, local(): lax.psum(shares[0].astype(jnp.bfloat16), 'seq').astype(jnp.float32)  84.5 us
  transfers between devices with their start and end apart: 23, of which 23 were waited for; matrix products, arithmetic and copies ran while one was open for 8% of the time, Pallas kernels for 0%

commit v1 on v0

--- a/solution.py
+++ b/solution.py
@@ -2,12 +2,28 @@
 import jax.numpy as jnp
 from jax import lax
 from jax.sharding import PartitionSpec as P
+from jax.lax import axis_index, axis_size, ppermute
 
 HEADS = 16
 HEAD_DIM = 64
 epsilon = 1e-06
 group_heads = 4
 highest = lax.Precision.HIGHEST
+
+
+def hold_teams_in(local_values, axis_name):
+    n_dev_all = axis_size(axis_name)
+    trail = [(dev_i, (dev_i + 1) % n_dev_all) for dev_i in range(n_dev_all)]
+    heap = [(dev_i, (dev_i - 1) % n_dev_all) for dev_i in range(n_dev_all)]
+    e_next, u1 = ([local_values], [local_values])
+    for _ in range(n_dev_all // 2):
+        e_next.append(ppermute(e_next[-1], axis_name, trail))
+    for _ in range((n_dev_all - 1) // 2):
+        u1.append(ppermute(u1[-1], axis_name, heap))
+    passed = jnp.concatenate([*e_next[::-1], *u1[1:]], axis=0)
+    return jnp.roll(
+        passed, shift=(axis_index(axis_name) - n_dev_all // 2) * local_values.shape[0], axis=0
+    )
 
 
 def modulated_norm(values, shift, scale):
@@ -133,7 +149,7 @@
         lax.all_gather(out_cross, "batch", axis=0, tiled=True),
         lax.all_gather(qkv_self, "batch", axis=0, tiled=True),
         lax.all_gather(out_self, "batch", axis=0, tiled=True),
-        lax.all_gather(mlp_in, "batch", axis=0, tiled=True),
+        hold_teams_in(mlp_in, "batch"),
         lax.all_gather(mlp_out, "batch", axis=0, tiled=True),
     )
     camera_gate = jax.nn.silu(camera.astype(jnp.float32)).astype(jnp.bfloat16)

time: 1940 us -> 1890 us (0.974)
  waiting for transfers between devices: 1620 us -> 1520 us
    ppermute x0 -> x7, waiting for transfers between devices: none -> 175 us  [the longest x4 175 us: hold_teams_in(): e_next.append(ppermute(e_next[-1], axis_name, trail))]
    all_gather x1 -> x0, waiting for transfers between devices: 122 us -> none  [local(): lax.all_gather(mlp_in, 'batch', axis=0, tiled=True)]
    all_gather x1, waiting for transfers between devices: 117 us -> 25 us  [local(): lax.all_gather(mlp_out, 'batch', axis=0, tiled=True)]
    reduce_scatter x1, waiting for transfers between devices: 35.5 us -> 4.59 us  [local(): lax.psum_scatter(key_terms.astype(jnp.bfloat16), 'seq', scatter_dimension...]
    reduce_scatter x1, waiting for transfers between devices: 5.37 us -> 35.7 us  [local(): lax.psum_scatter(value_terms.astype(jnp.bfloat16), 'seq', scatter_dimensi...]
    all_gather x1, waiting for transfers between devices: 24.1 us -> 0.01 us  [local(): lax.all_gather(out_self, 'batch', axis=0, tiled=True)]
    unnamed x123 -> x158, local copies, waits for them, and re-layouts: 5.86 us -> 27.4 us
    all_gather x1, waiting for transfers between devices: 20.9 us -> 0.01 us  [local(): lax.all_gather(value_local, 'seq', axis=0, tiled=True)]
  transfers between devices with their start and end apart: 23 -> 29, of which waited for: 23 -> 23; matrix products, arithmetic and copies ran while one was open for 8% -> 9% of each run, Pallas kernels for 0% -> 0%
where the time goes in v1:
time: 1890 us; the launch traced here: 1880 us
  waiting for transfers between devices  1520 us (80%)
  matrix products  206 us (11%)
  local copies, waits for them, and re-layouts  76.9 us (4%)
  other arithmetic  30.1 us (2%)
    ppermute x4, waiting for transfers between devices, hold_teams_in(): e_next.append(ppermute(e_next[-1], axis_name, trail))  175 us
    reduce_scatter x1, waiting for transfers between devices, local(): lax.psum_scatter(terms[6].astype(jnp.bfloat16), 'batch', scatter_dimensio...  152 us
    reduce_scatter x1, waiting for transfers between devices, local(): lax.psum_scatter(terms[5].astype(jnp.bfloat16), 'batch', scatter_dimensio...  152 us
    reduce_scatter x1, waiting for transfers between devices, local(): lax.psum_scatter(terms[3].astype(jnp.bfloat16), 'batch', scatter_dimensio...  121 us
    psum x1, waiting for transfers between devices, local(): grad_table = lax.psum(grad_table, ('batch', 'seq'))  119 us
    all_gather x1, waiting for transfers between devices, local(): lax.all_gather(qkv_self, 'batch', axis=0, tiled=True)  96.9 us
    psum x1, waiting for transfers between devices, local(): lax.psum(shares[0].astype(jnp.bfloat16), 'seq').astype(jnp.float32)  84.5 us
    reduce_scatter x1, waiting for transfers between devices, local(): lax.psum_scatter(terms[1].astype(jnp.bfloat16), 'batch', scatter_dimensio...  78 us
  transfers between devices with their start and end apart: 29, of which 23 were waited for; matrix products, arithmetic and copies ran while one was open for 9% of the time, Pallas kernels for 0%

profile of v1, /device:TPU:0, one launch (start us, length us, event | category | flops | bytes accessed | tf_op | source)
XLA Modules:
  0.0 1875.6 jit_solution(8187923995961469585)
XLA Ops:
  15.5 69.2 %all-reduce.5.cloned.1.call-done = f32[8,6144]{1,0:T(8,128)} async-done(((f32[8,6144]{1,0:T(8,128)}), f32[8,6144]{1,0:T(8,128)}) %all-reduce.5.cloned.1.call-update) | async-done | bytes 196624 | tf_op jit(solution)/shard_map/psum | solution.py:156
  85.7 49.7 %all-gather.9.cloned.1.call-done = bf16[1024,1024]{1,0:T(8,128)(2,1)} async-done(((bf16[128,1024]{1,0:T(8,128)(2,1)}), bf16[1024,1024]{1,0:T(8,128)(2,1)}) %all-gather.9.cloned.1.call-update) | async-done | bytes 2097168 | tf_op jit(solution)/shard_map/all_gather | solution.py:147
  138.0 58.8 %all-gather.11.cloned.1.call-done = bf16[768,2048]{1,0:T(8,128)(2,1)} async-done(((bf16[96,2048]{1,0:T(8,128)(2,1)}), bf16[768,2048]{1,0:T(8,128)(2,1)}) %all-gather.11.cloned.1.call-update) | async-done | bytes 3145744 | tf_op jit(solution)/shard_map/all_gather | solution.py:148
  249.9 96.9 %all-gather.15.cloned.1.call-done = bf16[1024,3072]{1,0:T(8,128)(2,1)} async-done(((bf16[128,3072]{1,0:T(8,128)(2,1)}), bf16[1024,3072]{1,0:T(8,128)(2,1)}) %all-gather.15.cloned.1.call-update) | async-done | bytes 6291472 | tf_op jit(solution)/shard_map/all_gather | solution.py:150
  354.3 26.7 %collective-permute-done = bf16[128,4096]{1,0:T(8,128)(2,1)} collective-permute-done((bf16[128,4096]{1,0:T(8,128)(2,1)}, bf16[128,4096]{1,0:T(8,128)(2,1)}, u32[]{:S(2)}, u32[]{:S(2)}) %collective-permute-start) | collective-permute-done | bytes 1048608 | tf_op jit(solution)/shard_map/ppermute | solution.py:20
  385.7 41.5 %collective-permute-done.1 = bf16[128,4096]{1,0:T(8,128)(2,1)S(1)} collective-permute-done((bf16[128,4096]{1,0:T(8,128)(2,1)}, bf16[128,4096]{1,0:T(8,128)(2,1)S(1)}, u32[]{:S(2)}, u32[]{:S(2)}) %collective-permute-start.1) | collective-permute-done | bytes 1048608 | tf_op jit(solution)/shard_map/ppermute | solution.py:20
  432.9 53.2 %collective-permute-done.2 = bf16[128,4096]{1,0:T(8,128)(2,1)} collective-permute-done((bf16[128,4096]{1,0:T(8,128)(2,1)S(1)}, bf16[128,4096]{1,0:T(8,128)(2,1)}, u32[]{:S(2)}, u32[]{:S(2)}) %collective-permute-start.2) | collective-permute-done | bytes 1048608 | tf_op jit(solution)/shard_map/ppermute | solution.py:20
  491.3 53.7 %collective-permute-done.3 = bf16[128,4096]{1,0:T(8,128)(2,1)} collective-permute-done((bf16[128,4096]{1,0:T(8,128)(2,1)}, bf16[128,4096]{1,0:T(8,128)(2,1)}, u32[]{:S(2)}, u32[]{:S(2)}) %collective-permute-start.3) | collective-permute-done | bytes 1048608 | tf_op jit(solution)/shard_map/ppermute | solution.py:20
  575.2 22.2 %while.57 = (s32[]{:T(128)}, bf16[4,4,256,64]{2,3,1,0:T(8,128)(2,1)}, f32[4,4,256,1]{2,1,3,0:T(4,128)S(1)}, f32[4,4,256,1]{2,1,3,0:T(4,128)S(1)}, bf16[4,4,256,6...) while((s32[]{:T(128)}, ...), condition=%wide.region_12.13_spmd, body=%wide.region_9.12_spmd.sunk | while | flops 277870592 | bytes 14063705 | solution.py:81
  608.9 25.0 %all-gather.23.cloned.1.call-done = bf16[4096,1024]{1,0:T(8,128)(2,1)} async-done(((bf16[512,1024]{1,0:T(8,128)(2,1)}), bf16[4096,1024]{1,0:T(8,128)(2,1)}) %all-gather.23.cloned.1.call-update) | async-done | bytes 8388624 | tf_op jit(solution)/shard_map/all_gather | solution.py:153
  657.4 47.9 %while.58 = (s32[]{:T(128)}, bf16[4,4,256,64]{2,3,1,0:T(8,128)(2,1)}, f32[4,4,1024,64]{2,3,1,0:T(8,128)}, f32[4,4,1024,64]{2,3,1,0:T(8,128)}, bf16[4,4,256,64]{2...) while((s32[]{:T(128)}, ...), condition=%wide.region_19.20_spmd, body=%wide.region_17.19_spmd.sunk | while | flops 680852480 | bytes 44340364 | solution.py:116
  706.2 42.0 %reduce-scatter.12.cloned.1.call-done = f32[256,1024]{0,1:T(8,128)} async-done(((f32[1024,1024]{0,1:T(8,128)}), f32[256,1024]{0,1:T(8,128)}) %reduce-scatter.12.cloned.1.call-update) | async-done | bytes 1048592 | tf_op jit(solution)/shard_map/reduce_scatter | solution.py:210
  749.5 45.8 %reduce-scatter.14.cloned.1.call-done = f32[256,1024]{0,1:T(8,128)} async-done(((f32[1024,1024]{0,1:T(8,128)}), f32[256,1024]{0,1:T(8,128)}) %reduce-scatter.14.cloned.1.call-update) | async-done | bytes 1048592 | tf_op jit(solution)/shard_map/reduce_scatter | solution.py:211
  808.6 46.1 %while.59 = (s32[]{:T(128)}, bf16[4,4,256,64]{2,3,1,0:T(8,128)(2,1)}, bf16[4,4,1025,64]{2,3,1,0:T(8,128)(2,1)}, bf16[4,4,1025,64]{2,3,1,0:T(8,128)(2,1)}, pred[1...) while((s32[]{:T(128)}, ...), condition=%wide.region_26.27_spmd, body=%wide.region_24.26_spmd.sunk | while | flops 682566912 | bytes 65885444 | solution.py:116
  888.0 35.7 %reduce-scatter.20.cloned.1.call-done = bf16[1025,256]{0,1:T(8,128)(2,1)} async-done(((bf16[1025,1024]{0,1:T(8,128)(2,1)}), bf16[1025,256]{0,1:T(8,128)(2,1)}) %reduce-scatter.20.cloned.1.call-update) | async-done | bytes 524816 | tf_op jit(solution)/shard_map/reduce_scatter | solution.py:228
  946.3 48.9 %reduce-scatter.28.cloned.1.call-done = bf16[128,1024]{1,0:T(8,128)(2,1)} async-done(((bf16[1024,1024]{1,0:T(8,128)(2,1)}), bf16[128,1024]{1,0:T(8,128)(2,1)}) %reduce-scatter.28.cloned.1.call-update) | async-done | bytes 262160 | tf_op jit(solution)/shard_map/reduce_scatter | solution.py:291
  995.1 71.2 %reduce-scatter.24.cloned.1.call-done = bf16[128,1024]{1,0:T(8,128)(2,1)} async-done(((bf16[1024,1024]{1,0:T(8,128)(2,1)}), bf16[128,1024]{1,0:T(8,128)(2,1)}) %reduce-scatter.24.cloned.1.call-update) | async-done | bytes 262160 | tf_op jit(solution)/shard_map/reduce_scatter | solution.py:285
  1066.3 71.1 %reduce-scatter.16.cloned.1.call-done = bf16[128,1024]{1,0:T(8,128)(2,1)} async-done(((bf16[1024,1024]{1,0:T(8,128)(2,1)}), bf16[128,1024]{1,0:T(8,128)(2,1)}) %reduce-scatter.16.cloned.1.call-update) | async-done | bytes 262160 | tf_op jit(solution)/shard_map/reduce_scatter | solution.py:279
  1137.4 152.0 %reduce-scatter.32.cloned.1.call-done = bf16[512,1024]{1,0:T(8,128)(2,1)} async-done(((bf16[4096,1024]{1,0:T(8,128)(2,1)}), bf16[512,1024]{1,0:T(8,128)(2,1)}) %reduce-scatter.32.cloned.1.call-update) | async-done | bytes 1048592 | tf_op jit(solution)/shard_map/reduce_scatter | solution.py:297
  1289.4 151.5 %reduce-scatter.30.cloned.1.call-done = bf16[128,4096]{1,0:T(8,128)(2,1)} async-done(((bf16[1024,4096]{1,0:T(8,128)(2,1)}), bf16[128,4096]{1,0:T(8,128)(2,1)}) %reduce-scatter.30.cloned.1.call-update) | async-done | bytes 1048592 | tf_op jit(solution)/shard_map/reduce_scatter | solution.py:294
  1441.0 78.0 %reduce-scatter.22.cloned.1.call-done = bf16[96,2048]{1,0:T(8,128)(2,1)} async-done(((bf16[768,2048]{1,0:T(8,128)(2,1)}), bf16[96,2048]{1,0:T(8,128)(2,1)}) %reduce-scatter.22.cloned.1.call-update) | async-done | bytes 393232 | tf_op jit(solution)/shard_map/reduce_scatter | solution.py:282
  1519.0 121.0 %reduce-scatter.26.cloned.1.call-done = bf16[128,3072]{1,0:T(8,128)(2,1)} async-done(((bf16[1024,3072]{1,0:T(8,128)(2,1)}), bf16[128,3072]{1,0:T(8,128)(2,1)}) %reduce-scatter.26.cloned.1.call-update) | async-done | bytes 786448 | tf_op jit(solution)/shard_map/reduce_scatter | solution.py:288
  1649.8 119.5 %all-reduce.7.cloned.1.call-done = f32[8,6144]{1,0:T(8,128)} async-done(((f32[8,6144]{1,0:T(8,128)}), f32[8,6144]{1,0:T(8,128)}) %all-reduce.7.cloned.1.call-update) | async-done | bytes 196624 | tf_op jit(solution)/shard_map/psum | solution.py:261
  1773.3 84.5 %all-reduce.9.cloned.1.call-done = (bf16[128,1024]{1,0:T(8,128)(2,1)}, bf16[96,2048]{1,0:T(8,128)(2,1)}, bf16[128,1024]{1,0:T(8,128)(2,1)}, bf16[128,3072]{1,0:T...) async-done(((bf16[128,1024]{1,0:T(8,128)(2,1)}, bf16[96,2048]{1,0:T(8,128)(2,1)}, bf16[128,1024]{1,0:T(8,128)(2,1)}, ...) | async-done | bytes 4063248 | tf_op jit(solution)/shard_map/psum | solution.py:302
  (442 shorter events, 372.6 us)
Async XLA Ops:
  7.2 77.5 %all-reduce.5.cloned.1.call-start = ((), (), s32[]{:S(2)}) async-start(), calls=%async_computation.11 | async-start | bytes 393216 | tf_op jit(solution)/shard_map/psum | solution.py:156
  9.8 125.6 %all-gather.9.cloned.1.call-start = ((), (), s32[]{:S(2)}) async-start(), calls=%async_computation.12 | async-start | bytes 2359296 | tf_op jit(solution)/shard_map/all_gather | solution.py:147
  10.6 186.2 %all-gather.11.cloned.1.call-start = ((), (), s32[]{:S(2)}) async-start(), calls=%async_computation.13 | async-start | bytes 3538944 | tf_op jit(solution)/shard_map/all_gather | solution.py:148
  11.3 235.6 %all-gather.13.cloned.1.call-start = ((), (), s32[]{:S(2)}) async-start(), calls=%async_computation.14 | async-start | bytes 2359296 | tf_op jit(solution)/shard_map/all_gather | solution.py:149
  11.9 334.9 %all-gather.15.cloned.1.call-start = ((), (), s32[]{:S(2)}) async-start(), calls=%async_computation.15 | async-start | bytes 7077888 | tf_op jit(solution)/shard_map/all_gather | solution.py:150
  12.5 554.0 %all-gather.17.cloned.1.call-start = ((), (), s32[]{:S(2)}) async-start(), calls=%async_computation.16 | async-start | bytes 2621440 | tf_op jit(solution)/shard_map/all_gather | solution.py:183
  352.7 217.7 %all-gather.19.cloned.1.call-start = ((), (), s32[]{:S(2)}) async-start(), calls=%async_computation.17 | async-start | bytes 2621440 | tf_op jit(solution)/shard_map/all_gather | solution.py:184
  353.5 243.9 %all-gather.21.cloned.1.call-start = ((), (), s32[]{:S(2)}) async-start(), calls=%async_computation.18 | async-start | bytes 2359296 | tf_op jit(solution)/shard_map/all_gather | solution.py:151
  354.2 279.7 %all-gather.23.cloned.1.call-start = ((), (), s32[]{:S(2)}) async-start(), calls=%async_computation.19 | async-start | bytes 9437184 | tf_op jit(solution)/shard_map/all_gather | solution.py:153
  486.1 58.9 %collective-permute-start.3 = (bf16[128,4096]{1,0:T(8,128)(2,1)}, bf16[128,4096]{1,0:T(8,128)(2,1)}, u32[]{:S(2)}, u32[]{:S(2)}) collective-permute-start(bf16[128,4096]{1,0:T(8,128)(2,1)} %collective-permute-done.2), channel_id=1, source_target_pairs={{0,4},{4,8},{8,12},{12,16},{16,20},{20,24},{24,28},{28,0},{1,5},{5... | collective-permute-start | bytes 3145736 | tf_op jit(solution)/shard_map/ppermute | solution.py:20
  488.7 259.5 %reduce-scatter.12.cloned.1.call-start = ((), (), s32[]{:S(2)}) async-start(), calls=%async_computation.20 | async-start | bytes 5242880 | tf_op jit(solution)/shard_map/reduce_scatter | solution.py:210
  488.9 62.9 %collective-permute-start.6 = (bf16[128,4096]{1,0:T(8,128)(2,1)}, bf16[128,4096]{1,0:T(8,128)(2,1)S(1)}, u32[]{:S(2)}, u32[]{:S(2)}) collective-permute-start(bf16[128,4096]{1,0:T(8,128)(2,1)} %collective-permute-done.5), channel_id=1, source_target_pairs={{0,28},{4,0},{8,4},{12,8},{16,12},{20,16},{24,20},{28,24},{1,29},{... | collective-permute-start | bytes 3145736 | tf_op jit(solution)/shard_map/ppermute | solution.py:22
  705.4 89.9 %reduce-scatter.14.cloned.1.call-start = ((), (), s32[]{:S(2)}) async-start(), calls=%async_computation.21 | async-start | bytes 5242880 | tf_op jit(solution)/shard_map/reduce_scatter | solution.py:211
  706.1 181.9 %reduce-scatter.18.cloned.1.call-start = ((), (), s32[]{:S(2)}) async-start(), calls=%async_computation.24 | async-start | bytes 2949120 | tf_op jit(solution)/shard_map/reduce_scatter | solution.py:225
  854.8 68.9 %reduce-scatter.20.cloned.1.call-start = ((), (), s32[]{:S(2)}) async-start(), calls=%async_computation.25 | async-start | bytes 2949120 | tf_op jit(solution)/shard_map/reduce_scatter | solution.py:228
  855.6 139.6 %reduce-scatter.28.cloned.1.call-start = ((), (), s32[]{:S(2)}) async-start(), calls=%async_computation.29 | async-start | bytes 2359296 | tf_op jit(solution)/shard_map/reduce_scatter | solution.py:291
  858.9 207.4 %reduce-scatter.24.cloned.1.call-start = ((), (), s32[]{:S(2)}) async-start(), calls=%async_computation.27 | async-start | bytes 2359296 | tf_op jit(solution)/shard_map/reduce_scatter | solution.py:285
  862.9 274.5 %reduce-scatter.16.cloned.1.call-start = ((), (), s32[]{:S(2)}) async-start(), calls=%async_computation.23 | async-start | bytes 2359296 | tf_op jit(solution)/shard_map/reduce_scatter | solution.py:279
  866.3 423.1 %reduce-scatter.32.cloned.1.call-start = ((), (), s32[]{:S(2)}) async-start(), calls=%async_computation.31 | async-start | bytes 9437184 | tf_op jit(solution)/shard_map/reduce_scatter | solution.py:297
  875.0 566.0 %reduce-scatter.30.cloned.1.call-start = ((), (), s32[]{:S(2)}) async-start(), calls=%async_computation.30 | async-start | bytes 9437184 | tf_op jit(solution)/shard_map/reduce_scatter | solution.py:294
  883.4 635.6 %reduce-scatter.22.cloned.1.call-start = ((), (), s32[]{:S(2)}) async-start(), calls=%async_computation.26 | async-start | bytes 3538944 | tf_op jit(solution)/shard_map/reduce_scatter | solution.py:282
  933.6 706.4 %reduce-scatter.26.cloned.1.call-start = ((), (), s32[]{:S(2)}) async-start(), calls=%async_computation.28 | async-start | bytes 7077888 | tf_op jit(solution)/shard_map/reduce_scatter | solution.py:288
  939.9 829.3 %all-reduce.7.cloned.1.call-start = ((), (), s32[]{:S(2)}) async-start(), calls=%async_computation.22 | async-start | bytes 393216 | tf_op jit(solution)/shard_map/psum | solution.py:261
  946.2 911.6 %all-reduce.9.cloned.1.call-start = ((), (), s32[]{:S(2)}) async-start(), calls=%async_computation.32 | async-start | bytes 8126464 | tf_op jit(solution)/shard_map/psum | solution.py:302
  (98 other events, 5431.7 us)
Sparse Core Ops, SparseCore 0:
  11.9 72.7 all-reduce.4
  87.1 48.3 all-gather.8
  137.9 58.9 all-gather.10
  199.0 47.8 all-gather.12
  249.2 97.5 all-gather.14
  352.8 20.7 all-gather.16
  375.9 22.5 all-gather.18
  400.8 81.8 all-gather.20
  488.9 144.9 all-gather.22
  705.5 42.6 reduce-scatter.11
  750.7 44.4 reduce-scatter.13
  854.9 33.0 reduce-scatter.17
  890.6 33.0 reduce-scatter.19
  927.5 67.5 reduce-scatter.27
  999.5 66.8 reduce-scatter.23
  1070.7 66.6 reduce-scatter.15
  1141.3 148.0 reduce-scatter.31
  1292.9 148.0 reduce-scatter.29
  1445.5 73.4 reduce-scatter.21
  1522.8 117.0 reduce-scatter.25
  1647.0 122.1 all-reduce.6
  1772.3 85.3 all-reduce.8
